TPU v7x, 128 devices: a whole 4x4x4 slice. The times are simulated.
128 devices in a mesh: row: 16 (over x, z_lo, core), rhs: 8 (over y, z_hi).
Axes of the slice: x: 4, y: 4, z: 4 (z_hi: 2, z_lo: 2; z = z_hi * 2 + z_lo), core: 2. Of those that a mesh axis runs over, the one named last changes fastest.
Arguments:
- right_sides: float32 [32768, 8192], P('row', 'rhs'), may hold values from -6 to 6
- panel_diag: float32 [2, 512, 512], replicated, as said below
- left_factor: bfloat16 [32768, 2, 512], P('row', None, 'rhs'), may hold values from -0.25 to 0.25
- right_factor: bfloat16 [32768, 2, 512], P('row', None, 'rhs'), may hold values from -0.25 to 0.25
- tile_scale: float32 [64, 2], P('row'), may hold values from 0.3 to 1.5
- tile_rank: int32 [64, 2], P('row'), may hold values from 128 to 512, as said below
Outputs:
- solved: float32 [32768, 8192], P('row', 'rhs')
Inputs may be any that keep to these rules, and one draw needn't show every extreme that they name: panel_diag[k] is lower triangular with diagonal entries of 1 or more. `tile_rank`: every rank is a multiple of 128; some block has rank 512 in both panels.
All inputs are finite; a program needn't handle non-finite values.
Results may differ from a plain program's by a relative error of at most 0.0003.
Values may be sent and summed in bfloat16 or wider, within the bound.
No kernel may reach another device: no remote copies, remote signals or barrier semaphores. Data moves between devices by JAX's collectives and lax.ppermute only.
A program may use at most 128 MiB of HBM per device.

v0:
```python
import jax
import jax.numpy as jnp
from jax import lax
from jax.sharding import PartitionSpec as P


def filled_up(lines, size):
    spare = -lines.shape[0] % size
    if not spare:
        return lines
    return jnp.concatenate([lines, jnp.zeros((spare, *lines.shape[1:]), lines.dtype)])


def broadcast_by_parts(shard, axis, root):
    lines = jnp.where(lax.axis_index(axis) == root, shard, jnp.zeros_like(shard)).reshape(
        -1, *shard.shape[1:][-1:]
    )
    padded = filled_up(lines, lax.axis_size(axis))
    own = lax.psum_scatter(padded, axis, scatter_dimension=0, tiled=True)
    return lax.all_gather(own, axis, axis=0, tiled=True)[: len(lines)].reshape(shard.shape)


def spread(value, axis, source):
    kept = jnp.where(lax.axis_index(axis) == source, value, 0).astype(value.dtype)
    return lax.psum(kept, axis)


def solve_panel(triangle, target):
    return lax.linalg.triangular_solve(triangle, target, left_side=True, lower=True)


def send_second(solution):
    return broadcast_by_parts(solution, "row", 1)


def shards(right_sides, panel_diag, left_factor, right_factor, tile_scale, tile_rank):
    row_count, column_count = right_sides.shape
    panel_rows = panel_diag.shape[1]
    block_count = row_count // panel_rows
    row_index = lax.axis_index("row")
    global_block = jnp.arange(block_count, dtype=jnp.int32) * lax.axis_size("row") + row_index
    columns = jnp.arange(panel_rows, dtype=jnp.int32)
    blocks = right_sides.reshape(block_count, panel_rows, column_count)
    weights = []
    for panel_index in range(2):
        active = jnp.where(global_block > panel_index, tile_scale[:, panel_index], 0.0)
        weights.append(
            active[:, None]
            * (columns[None, :] < tile_rank[:, panel_index : panel_index + 1]).astype(jnp.float32)
        )
    left_full, right_full = (
        lax.all_gather(left_factor, "rhs", axis=2, tiled=True),
        lax.all_gather(right_factor, "rhs", axis=2, tiled=True),
    )
    left_blocks = left_full.reshape(block_count, panel_rows, 2, panel_rows)
    right_blocks = right_full.reshape(block_count, panel_rows, 2, panel_rows)

    def apply_panel(panel_index, solution, current, chosen):
        inner = jnp.einsum(
            "lqr,qn->lrn",
            right_blocks[chosen, :, panel_index, :],
            solution,
            precision=lax.Precision.HIGH,
            preferred_element_type=jnp.float32,
        )
        inner = inner * weights[panel_index][chosen][:, :, None]
        return current[chosen] - jnp.einsum(
            "lpr,lrn->lpn",
            left_blocks[chosen, :, panel_index, :],
            inner,
            precision=lax.Precision.HIGH,
            preferred_element_type=jnp.float32,
        )

    first_local = solve_panel(panel_diag[0], blocks[0])
    first_solution = spread(first_local, "row", 0)
    leading = apply_panel(0, first_solution, blocks, slice(0, 1))
    second_local = solve_panel(panel_diag[1], leading[0])
    second_solution = send_second(second_local)
    trailing = apply_panel(0, first_solution, blocks, slice(1, None))
    blocks = jnp.concatenate([leading, trailing], axis=0)
    blocks = apply_panel(1, second_solution, blocks, slice(None))
    leading_block = jnp.where(
        row_index == 0, first_solution, jnp.where(row_index == 1, second_solution, blocks[0])
    )
    blocks = jnp.concatenate([leading_block[None], blocks[1:]], axis=0)
    return blocks.reshape(row_count, column_count)


def solution(mesh):
    placed = (
        P("row", "rhs"),
        P(),
        P("row", None, "rhs"),
        P("row", None, "rhs"),
        P("row", None),
        P("row", None),
    )
    return jax.shard_map(
        shards, mesh=mesh, in_specs=placed, out_specs=P("row", "rhs"), check_vma=False
    )
```

profile of v0, /device:TPU:1, one launch (start us, length us, event | category | flops | bytes accessed | tf_op | source)
XLA Modules:
  0.0 371.6 jit_solution(11841647041793418647)
XLA Ops:
  7.4 2.4 copy.14
  9.8 0.7 all-gather.6.cloned.1.call-update
  10.6 1.8 bitcast_select_fusion
  12.4 8.2 %while.4 = (s32[]{:T(128)}, f32[512,512]{1,0:T(8,128)S(1)}, s32[4,2]{0,1:T(2,128)S(1)}, f32[4,128,128]{2,1,0:T(8,128)S(1)}, s32[]{:T(128)}) while((s32[]{:T(128)}, f32[512,512]{1,0:T(8,128)S(1)}, s32[4,2]{0,1:T(2,128)S(1)}, f32[4,128,128]{2,1,0:T(8,128)S(1)}, s32[]{:T(128)}) %tuple.38), condition=%wide.while_cond, body=%wide.while_body.sunk | while | flops 2 | bytes 131189 | solution.py:29
  12.5 0.6 fusion.86
  13.1 1.4 bitcast_dynamic-update-slice_fusion.4
  14.5 0.1 constant_dynamic-slice_fusion.4
  14.6 0.6 fusion.86
  15.1 1.4 bitcast_dynamic-update-slice_fusion.4
  16.6 0.6 fusion.86
  17.2 1.4 bitcast_dynamic-update-slice_fusion.4
  18.6 0.6 fusion.86
  19.2 1.4 bitcast_dynamic-update-slice_fusion.4
  20.6 39.3 %custom-call.4 = f32[4,128,128]{1,2,0:T(8,128)S(1)} custom-call(f32[4,128,128]{2,1,0:T(8,128)S(1)} %get-tuple-element.20), custom_call_target="InvertDiagBlocksLowerTriangular" | custom-call | tf_op jit(solution)/shard_map/triangular_solve/custom-call.1 | solution.py:29
  59.9 1.7 fusion.51
  61.6 1.6 convolution_subtract_fusion.3
  63.2 0.6 fusion.64
  63.9 1.8 convolution_subtract_fusion.1
  65.7 0.6 fusion.62
  66.3 2.1 fusion.38
  68.5 0.6 fusion.61
  69.1 1.6 maximum_select_fusion
  70.7 0.2 reduce-scatter.2.cloned.1.call-start
  70.9 0.4 copy-done.9
  71.4 7.5 %while.5 = (s32[]{:T(128)}, f32[512,512]{1,0:T(8,128)S(1)}, s32[4,2]{0,1:T(2,128)S(1)}, f32[4,128,128]{2,1,0:T(8,128)S(1)}, s32[]{:T(128)}) while((s32[]{:T(128)}, f32[512,512]{1,0:T(8,128)S(1)}, s32[4,2]{0,1:T(2,128)S(1)}, f32[4,128,128]{2,1,0:T(8,128)S(1)}, s32[]{:T(128)}) %tuple.54), condition=%wide.while_cond.clone, body=%wide.while_body.clone.sunk | while | flops 2 | bytes 131189 | solution.py:29
  71.5 0.5 fusion.87
  72.1 1.3 bitcast_dynamic-update-slice_fusion.5
  73.4 0.5 fusion.87
  73.9 1.3 bitcast_dynamic-update-slice_fusion.5
  75.3 0.5 fusion.87
  75.8 1.3 bitcast_dynamic-update-slice_fusion.5
  77.2 0.5 fusion.87
  77.7 1.3 bitcast_dynamic-update-slice_fusion.5
  79.0 39.3 %custom-call.5 = f32[4,128,128]{1,2,0:T(8,128)S(1)} custom-call(f32[4,128,128]{2,1,0:T(8,128)S(1)} %get-tuple-element.21), custom_call_target="InvertDiagBlocksLowerTriangular" | custom-call | tf_op jit(solution)/shard_map/triangular_solve/custom-call.1 | solution.py:29
  118.3 11.2 %copy.15 = bf16[2048,2,512]{2,0,1:T(8,128)(2,1)} copy(bf16[2048,2,512]{0,1,2:T(2,128)(2,1)} %all-gather.4.cloned.1.call-done) | data formatting | bytes 8388608 | tf_op jit(solution)/shard_map/all_gather | solution.py:53
  129.6 30.4 %all-gather.6.cloned.1.call-done = bf16[2048,2,512]{0,2,1:T(8,128)(2,1)} async-done(((bf16[2048,2,64]{0,2,1:T(8,128)(2,1)}), bf16[2048,2,512]{0,2,1:T(8,128)(2,1)}) %all-gather.6.cloned.1.call-update) | async-done | bytes 4194320 | tf_op jit(solution)/shard_map/all_gather | solution.py:52
  160.0 6.2 %copy.16 = bf16[2048,2,512]{2,0,1:T(8,128)(2,1)} copy(bf16[2048,2,512]{0,2,1:T(8,128)(2,1)} %all-gather.6.cloned.1.call-done) | data formatting | bytes 8388608 | tf_op jit(solution)/shard_map/all_gather | solution.py:52
  166.2 50.8 %all-reduce.2.cloned.1.call-done = f32[512,1024]{1,0:T(8,128)} async-done(((f32[512,1024]{1,0:T(8,128)}), f32[512,1024]{1,0:T(8,128)}) %all-reduce.2.cloned.1.call-update) | async-done | bytes 2097168 | tf_op jit(solution)/shard_map/psum | solution.py:25
  217.0 3.0 fusion.50
  220.0 3.1 bitcast_subtract_fusion.1
  223.2 0.6 fusion.48
  223.8 0.6 convolution_subtract_fusion.2
  224.4 0.6 fusion.60
  225.1 0.7 convolution_subtract_fusion
  225.8 0.6 fusion.58
  226.4 1.1 fusion.35
  227.5 0.6 fusion.57
  228.2 1.6 maximum_select_fusion.1
  229.8 0.3 all-gather.8.cloned.1.call-start
  230.0 61.5 %reduce-scatter.2.cloned.1.call-done = f32[32,1024]{1,0:T(8,128)} async-done(((f32[512,1024]{1,0:T(8,128)}), f32[32,1024]{1,0:T(8,128)}) %reduce-scatter.2.cloned.1.call-update) | async-done | bytes 131088 | tf_op jit(solution)/shard_map/reduce_scatter | solution.py:19
  291.6 0.7 copy-done.8
  292.4 1.4 copy-done.2
  293.8 0.7 copy-done.4
  294.5 3.5 fusion.17
  298.0 7.2 %bitcast_subtract_fusion = f32[3,512,1024]{2,1,0:T(8,128)} fusion(f32[3,512,1024]{2,1,0:T(8,128)S(1)} %bitcast.121, f32[1024,3,512]{2,0,1:T(8,128)S(1)} %fusion.17, f32[3,512]{1,0:T(4,128)S(1)} %slice.186, bf16[4,512,2,512]{3,1,0,2:T(8,128)(2,1)} %bitcast.127), kind=kOutput, calls=%fused_computation.9 | convolution fusion | flops 4834983936 | bytes 20453376 | tf_op jit(solution)/shard_map/lpr,lrn->lpn/dot_general | solution.py:67
  305.2 24.0 %all-gather.8.cloned.1.call-done = f32[512,1024]{1,0:T(8,128)} async-done(((f32[32,1024]{1,0:T(8,128)}), f32[512,1024]{1,0:T(8,128)}) %all-gather.8.cloned.1.call-update) | async-done | bytes 2097168 | tf_op jit(solution)/shard_map/all_gather | solution.py:20
  329.2 10.3 %fusion.15 = f32[1024,4,512]{2,0,1:T(8,128)} fusion(bf16[4,512,2,512]{3,1,0,2:T(8,128)(2,1)} %bitcast.123, f32[512,1024]{1,0:T(8,128)} %all-gather.8.cloned.1.call-done), kind=kOutput, calls=%fused_computation.21 | convolution fusion | flops 6442450944 | bytes 12582912 | tf_op jit(solution)/shard_map/lqr,qn->lrn/dot_general | solution.py:59
  339.6 12.8 %maximum_subtract_fusion = f32[4,512,1024]{2,1,0:T(8,128)} fusion(f32[3,512,1024]{2,1,0:T(8,128)S(1)} %copy-done.1, f32[1,512,1024]{2,1,0:T(8,128)} %bitcast.125, f32[1024,4,512]{2,0,1:T(8,128)} %fusion.15, f32[4,512]{1,0:T(4,128)S(1)} %fusion.66, bf16[4,512,2,512]{3,1,0,2:T(8,128)(2,1)} %bitcast.128), kind=kOutput, calls=%fused_computation.4 | convolution fusion | flops 6448742400 | bytes 27271168 | tf_op jit(solution)/shard_map/lpr,lrn->lpn/dot_general | solution.py:67
  352.4 3.4 copy-done
  355.8 0.6 copy-done.5
  356.4 0.6 copy-done.6
  357.0 0.7 fusion.14
  357.7 2.1 slice-done
  359.8 4.2 %pad_maximum_fusion = f32[4,512,1024]{2,1,0:T(8,128)} fusion(f32[3,512,1024]{2,1,0:T(8,128)S(1)} %slice-done, f32[1,512,1024]{2,1,0:T(8,128)S(1)} %fusion.14), kind=kLoop, calls=%fused_computation.5 | loop fusion | flops 2097152 | bytes 16777216 | tf_op jit(solution)/shard_map/concatenate | solution.py:86
  (44 shorter events, 0.9 us)
Async XLA Ops:
  7.4 111.0 %all-gather.4.cloned.1.call-start = ((), (), s32[]{:S(2)}) async-start(), calls=%async_computation.2 | async-start | bytes 4718592 | tf_op jit(solution)/shard_map/all_gather | solution.py:53
  9.8 150.2 %all-gather.6.cloned.1.call-start = ((), (), s32[]{:S(2)}) async-start(), calls=%async_computation.3 | async-start | bytes 4718592 | tf_op jit(solution)/shard_map/all_gather | solution.py:52
  10.5 206.5 %all-reduce.2.cloned.1.call-start = ((), (), s32[]{:S(2)}) async-start(), calls=%async_computation.1 | async-start | bytes 4194304 | tf_op jit(solution)/shard_map/psum | solution.py:25
  70.6 0.7 copy-start.9
  70.7 0.7 copy-start.10
  70.7 220.9 %reduce-scatter.2.cloned.1.call-start = ((), (), s32[]{:S(2)}) async-start(), calls=%async_computation.4 | async-start | bytes 2228224 | tf_op jit(solution)/shard_map/reduce_scatter | solution.py:19
  71.4 58.1 %copy-start.7 = (f32[4,512]{1,0:T(4,128)}, f32[4,512]{1,0:T(4,128)S(1)}, u32[]{:S(2)}) copy-start(f32[4,512]{1,0:T(4,128)S(1)} %fusion.65) | copy-start | bytes 24580
  217.0 3.0 slice-start.2
  223.2 3.3 copy-start.3
  229.8 99.5 %all-gather.8.cloned.1.call-start = ((), (), s32[]{:S(2)}) async-start(), calls=%async_computation.5 | async-start | bytes 2228224 | tf_op jit(solution)/shard_map/all_gather | solution.py:20
  291.6 0.7 copy-start.8
  291.6 2.2 copy-start.2
  291.6 2.9 copy-start.4
  294.5 3.6 slice-start.1
  329.2 10.3 %copy-start.1 = (f32[3,512,1024]{2,1,0:T(8,128)S(1)}, f32[3,512,1024]{2,1,0:T(8,128)}, u32[]{:S(2)}) copy-start(f32[3,512,1024]{2,1,0:T(8,128)} %bitcast_subtract_fusion) | copy-start | bytes 18874372
  352.4 3.4 copy-start
  352.4 4.0 %copy-start.5 = (f32[512,1024]{1,0:T(8,128)S(1)}, f32[512,1024]{1,0:T(8,128)}, u32[]{:S(2)}) copy-start(f32[512,1024]{1,0:T(8,128)} %all-reduce.2.cloned.1.call-done) | copy-start | bytes 6291460
  352.4 4.6 %copy-start.6 = (f32[512,1024]{1,0:T(8,128)S(1)}, f32[512,1024]{1,0:T(8,128)}, u32[]{:S(2)}) copy-start(f32[512,1024]{1,0:T(8,128)} %all-gather.8.cloned.1.call-done) | copy-start | bytes 6291460
  357.0 2.8 slice-start
Sparse Core Ops, SparseCore 0:
  10.5 74.8 all-gather.3
  87.8 72.1 all-gather.5
Sparse Core Ops, SparseCore 1:
  70.8 146.2 all-reduce.1
  229.8 61.7 reduce-scatter.1
  293.1 36.0 all-gather.7
where the time goes:
time: 373 us; the launch traced here: 372 us
  waiting for transfers between devices  168 us (45%)
  other arithmetic  88.6 us (24%)
  matrix products  54 us (14%)
  local copies, waits for them, and re-layouts  45.4 us (12%)
  between operations  15.3 us (4%)
    another operation x4, other arithmetic, solve_panel(): lax.linalg.triangular_solve(triangle, target, left_side=True, lower=True)  80.4 us
    reduce_scatter x1, waiting for transfers between devices, broadcast_by_parts(): own = lax.psum_scatter(padded, axis, scatter_dimension=0, tiled=True)  61.5 us
    psum x1, waiting for transfers between devices, spread(): return lax.psum(kept, axis)  50.8 us
    all_gather x1, waiting for transfers between devices, shards(): lax.all_gather(left_factor, 'rhs', axis=2, tiled=True)  30.4 us
    all_gather x1, waiting for transfers between devices, broadcast_by_parts(): lax.all_gather(own, axis, axis=0, tiled=True)[:len(lines)]  24 us
    dot_general x3, matrix products, apply_panel(): jnp.einsum('lpr,lrn->lpn', left_blocks[chosen, :, panel_index, :], inner,...  23.1 us
    dot_general x3, matrix products, apply_panel(): jnp.einsum('lqr,qn->lrn', right_blocks[chosen, :, panel_index, :], soluti...  16.8 us
    another operation x27, local copies, waits for them, and re-layouts, solve_panel(): lax.linalg.triangular_solve(triangle, target, left_side=True, lower=True)  15.6 us
  transfers between devices with their start and end apart: 5, of which 4 were waited for; matrix products, arithmetic and copies ran while one was open for 36% of the time, Pallas kernels for 0%

commit v1 on v0

v1 whole, which is shorter than its diff:
```python
import functools

import jax
import jax.numpy as jnp
from jax import lax
from jax.experimental import pallas as pl
from jax.experimental.pallas import tpu as pltpu
from jax.sharding import PartitionSpec as P


SIZE = 512
TILE = 128
HALF = 64
STEP = 512
BOTH = ("row", "rhs")
NX, NL, NC, NY, NH = 4, 2, 2, 4, 2
F32, BF16 = jnp.float32, jnp.bfloat16


def flat(x, low, core, y, high):
    return ((x % NX) * 4 + (low % NL) * 2 + core % NC) * 8 + (y % NY) * 2 + high % NH


def moves(shift, keep):
    pairs = []
    for x in range(NX):
        for low in range(NL):
            for core in range(NC):
                for y in range(NY):
                    for high in range(NH):
                        place = (x, low, core, y, high)
                        if keep is None or keep(*place[:3]):
                            pairs.append((flat(*place), flat(*(a + b for a, b in zip(place, shift)))))
    return pairs


def shifted(value, x=0, low=0, core=0, y=0, high=0, keep=None):
    return lax.ppermute(value, BOTH, moves((x, low, core, y, high), keep))


def dot(a, b):
    return lax.dot_general(a, b, (((1,), (0,)), ((), ())), preferred_element_type=F32)


def dot_exact(a, b):
    return lax.dot_general(
        a, b, (((1,), (0,)), ((), ())), precision=lax.Precision.HIGHEST, preferred_element_type=F32
    )


def halves(value):
    high = value.astype(BF16)
    return high, (value - high.astype(F32)).astype(BF16)


def dot_split(a, b):
    a_high, a_low = halves(a)
    b_high, b_low = halves(b)
    return dot(a_high, b_high) + (dot(a_high, b_low) + dot(a_low, b_high))


def weight(place_ref, scale_ref, rank_ref, block, panel, shift):
    shard = lax.rem(place_ref[3] + shift[0], NY) * 2 + lax.rem(place_ref[4] + shift[1], NH)
    live = (block * (NX * NL * NC) + place_ref[5] > panel) & (shard * 64 < rank_ref[panel, block])
    return jnp.where(live, scale_ref[panel, block], 0.0)


SCALARS = pl.BlockSpec(memory_space=pltpu.SMEM)
PARAMS = pltpu.CompilerParams(vmem_limit_bytes=67_043_328)


def invert_kernel(d_ref, o_ref):
    o_ref[...] = jnp.zeros_like(o_ref)
    row = lax.broadcasted_iota(jnp.int32, (HALF, TILE), 0)
    lane = lax.broadcasted_iota(jnp.int32, (HALF, TILE), 1)
    left, col = lane < HALF, lane % HALF
    left_rows = lax.broadcasted_iota(jnp.int32, (8, TILE), 1) < HALF
    tile_row = lax.broadcasted_iota(jnp.int32, (TILE, TILE), 0)
    tile_lane = lax.broadcasted_iota(jnp.int32, (TILE, TILE), 1)
    work = []
    for t in range(SIZE // TILE):
        for p in range(2):
            span = slice(t * TILE, t * TILE + TILE)
            lower = d_ref[p, span, span]
            both = jnp.where(left, lower[:HALF], lower[HALF:])
            lanes = 1.0 / jnp.sum(jnp.where(row == col, both, 0.0), axis=0, keepdims=True)
            rows = 1.0 / jnp.sum(jnp.where(tile_row == tile_lane, lower, 0.0), axis=1, keepdims=True)
            unit = jnp.where(row > col, both * lanes, 0.0)
            start = jnp.where(row == col, 1.0, 0.0).astype(F32)
            strips = range(0, HALF, 8)
            work.append((p, span, rows, [unit[b : b + 8] for b in strips], [start[b : b + 8] for b in strips]))
    for i in range(HALF - 1):
        for _, _, _, unit, state in work:
            pivot = state[i // 8][i % 8 : i % 8 + 1, :]
            for b in range((i + 1) // 8, HALF // 8):
                column = jnp.where(left_rows, unit[b][:, i : i + 1], unit[b][:, HALF + i : HALF + i + 1])
                state[b] = state[b] - column * pivot
    for p, span, rows, _, state in work:
        both = jnp.concatenate(state, axis=0)
        inverse = jnp.concatenate([jnp.where(left, both, 0.0), jnp.where(left, 0.0, both)], axis=0) * rows
        below = jnp.where((tile_row >= HALF) & (tile_lane < HALF), d_ref[p, span, span], 0.0)
        o_ref[p, span, span] = inverse - dot_exact(inverse, dot_exact(below, inverse))
    for size in (TILE, 2 * TILE):
        for base in range(0, SIZE, 2 * size):
            for p in range(2):
                first, second = slice(base, base + size), slice(base + size, base + 2 * size)
                inner = dot_exact(d_ref[p, second, first], o_ref[p, first, first])
                o_ref[p, second, first] = -dot_exact(o_ref[p, second, second], inner)


def inverses(panel_diag):
    return pl.pallas_call(
        invert_kernel,
        out_shape=jax.ShapeDtypeStruct(panel_diag.shape, F32),
        name="inverses",
        compiler_params=PARAMS,
        cost_estimate=pl.CostEstimate(flops=2_000_000_000, bytes_accessed=4 << 20, transcendentals=0),
    )(panel_diag)


def ring_rows(place_ref, k):
    return pl.ds(pl.multiple_of(lax.rem(place_ref[0] + k, 4) * TILE, TILE), TILE)


def first_kernel(place_ref, inverse, *refs):
    quarters, o_ref, d_ref, right_ref, x_ref, sems = refs[:4], *refs[4:]

    @pl.when(place_ref[2] == 0)
    def _():
        loads = [pltpu.make_async_copy(inverse.at[0], d_ref, sems.at[4])]
        for k in range(4):
            loads.append(pltpu.make_async_copy(quarters[k], right_ref.at[ring_rows(place_ref, k)], sems.at[k]))
        for load in loads:
            load.start()
        for load in loads:
            load.wait()
        x_ref[...] = dot_split(d_ref[...], right_ref[...])
        store = pltpu.make_async_copy(x_ref, o_ref, sems.at[5])
        store.start()
        store.wait()


def first_solution(place, inverse, quarters):
    width = quarters[0].shape[1]
    there = pl.BlockSpec(memory_space=pltpu.HBM)
    return pl.pallas_call(
        first_kernel,
        in_specs=[SCALARS] + [there] * 5,
        out_specs=there,
        out_shape=jax.ShapeDtypeStruct((SIZE, width), F32),
        scratch_shapes=[
            pltpu.VMEM((SIZE, SIZE), F32),
            pltpu.VMEM((SIZE, width), F32),
            pltpu.VMEM((SIZE, width), F32),
            pltpu.SemaphoreType.DMA((6,)),
        ],
        name="first_solution",
        compiler_params=PARAMS,
        cost_estimate=pl.CostEstimate(flops=1_600_000_000, bytes_accessed=5 << 20, transcendentals=0),
    )(place, inverse, *quarters)


def place_kernel(place_ref, *refs):
    quarters, o_ref, buffer, sems = refs[:4], refs[4], refs[5], refs[6]

    @pl.when(place_ref[2] == 1)
    def _():
        loads, stores = [], []
        for k in range(4):
            loads.append(pltpu.make_async_copy(quarters[k], buffer.at[k], sems.at[k]))
            stores.append(pltpu.make_async_copy(buffer.at[k], o_ref.at[ring_rows(place_ref, k)], sems.at[4 + k]))
        for load in loads:
            load.start()
        for load, store in zip(loads, stores):
            load.wait()
            store.start()
        for store in stores:
            store.wait()


def put_in_place(place, quarters):
    width = quarters[0].shape[1]
    there = pl.BlockSpec(memory_space=pltpu.HBM)
    return pl.pallas_call(
        place_kernel,
        in_specs=[SCALARS] + [there] * 4,
        out_specs=there,
        out_shape=jax.ShapeDtypeStruct((SIZE, width), F32),
        scratch_shapes=[pltpu.VMEM((4, TILE, width), F32), pltpu.SemaphoreType.DMA((8,))],
        name="placed",
        compiler_params=PARAMS,
        cost_estimate=pl.CostEstimate(flops=0, bytes_accessed=4 << 20, transcendentals=0),
    )(place, *quarters)


def second_kernel(shifts, place_ref, scale_ref, rank_ref, d_ref, b_ref, *refs):
    near, pieces, outs = refs[:4], refs[4:-4], refs[-4:]

    @pl.when(place_ref[5] == 1)
    def _():
        first = jnp.concatenate([quarter[...] for quarter in near], axis=0)
        x_high, x_low = halves(dot_split(d_ref[0], first))
        parts = [piece[SIZE * h : SIZE * h + SIZE] for piece in pieces for h in range(2)]
        wide = lambda part, base: jnp.concatenate([part[base + 64 * t : base + 64 * t + 64] for t in range(4)], axis=1)
        left = jnp.concatenate([wide(part, 0) for part in parts], axis=0)
        inner = dot(left, x_high) + dot(left, x_low)
        scaled = [
            halves(inner[64 * j : 64 * j + 64] * weight(place_ref, scale_ref, rank_ref, 0, 0, shifts[j]))
            for j in range(8)
        ]
        right = jnp.concatenate([wide(part, 256) for part in parts], axis=0).T
        change = dot(right, jnp.concatenate([high for high, _ in scaled], axis=0)) + dot(
            right, jnp.concatenate([low for _, low in scaled], axis=0)
        )
        solved = dot_split(d_ref[1], b_ref[...] - change)
        for k in range(4):
            outs[k][...] = solved[TILE * k : TILE * k + TILE]


def second_solution(scalars, shifts, inverse, near, right_sides, pieces):
    width = right_sides.shape[1]
    quarter = pl.BlockSpec((TILE, STEP), lambda n: (0, n))
    return pl.pallas_call(
        functools.partial(second_kernel, shifts),
        grid=(width // STEP,),
        in_specs=[SCALARS] * 3
        + [
            pl.BlockSpec((2, SIZE, SIZE), lambda n: (0, 0, 0)),
            pl.BlockSpec((SIZE, STEP), lambda n: (0, n)),
        ]
        + [quarter] * 4
        + [pl.BlockSpec((2 * SIZE, TILE), lambda n: (0, 0)) for _ in pieces],
        out_specs=[quarter] * 4,
        out_shape=[jax.ShapeDtypeStruct((TILE, width), F32)] * 4,
        name="second_solution",
        compiler_params=PARAMS,
        cost_estimate=pl.CostEstimate(flops=4_000_000_000, bytes_accessed=9 << 20, transcendentals=0),
    )(*scalars, inverse, right_sides, *near, *pieces)


def update_kernel(panel, shifts, place_ref, scale_ref, rank_ref, b_ref, *refs):
    blocks, rest = refs[:8], refs[8:]
    sources, (o_ref, x_ref, high_ref, low_ref, sem) = rest[:-5], rest[-5:]
    block = pl.program_id(0)
    core, row = place_ref[2], place_ref[5]
    chosen = [core == panel, core == 1 - panel]

    @pl.when(block == 0)
    def _():
        for test, source in zip(chosen, sources):

            @pl.when(test)
            def _():
                copy = pltpu.make_async_copy(source, x_ref, sem)
                copy.start()
                copy.wait()

        high, rest = halves(x_ref[...])
        high_ref[...] = high
        low_ref[...] = rest

    @pl.when((block == 0) & (row == panel))
    def _():
        o_ref[...] = x_ref[...]

    @pl.when((block == 0) & (row == 1 - panel))
    def _():
        o_ref[...] = b_ref[...]

    @pl.when((block > 0) | (row > 1))
    def _():
        pieces = [ref[0] for ref in blocks]
        base = HALF * panel
        left = jnp.concatenate(
            [
                jnp.concatenate([piece[TILE * t + base : TILE * t + base + HALF] for t in range(4)], axis=1)
                for piece in pieces
            ],
            axis=0,
        )
        inner = dot(left, high_ref[...]) + dot(left, low_ref[...])
        scaled = [
            halves(
                inner[HALF * j : HALF * j + HALF] * weight(place_ref, scale_ref, rank_ref, block, panel, shifts[j])
            )
            for j in range(8)
        ]
        right = jnp.concatenate([piece[SIZE:, base : base + HALF] for piece in pieces], axis=1)
        change = [dot(right, jnp.concatenate([pair[part] for pair in scaled], axis=0)) for part in range(2)]
        o_ref[...] = b_ref[...] - (change[0] + change[1])


def update(panel, scalars, shifts, current, pieces, sources):
    rows, width = current.shape
    part = pl.BlockSpec((SIZE, width), lambda l: (l, 0))
    return pl.pallas_call(
        functools.partial(update_kernel, panel, shifts),
        grid=(rows // SIZE,),
        in_specs=[SCALARS] * 3
        + [part]
        + [pl.BlockSpec((1, 2 * SIZE, TILE), lambda l: (l, 0, 0)) for _ in pieces]
        + [pl.BlockSpec(memory_space=pltpu.HBM) for _ in sources],
        out_specs=part,
        out_shape=jax.ShapeDtypeStruct((rows, width), F32),
        scratch_shapes=[
            pltpu.VMEM((SIZE, width), F32),
            pltpu.VMEM((SIZE, width), BF16),
            pltpu.VMEM((SIZE, width), BF16),
            pltpu.SemaphoreType.DMA(()),
        ],
        compiler_params=PARAMS,
        cost_estimate=pl.CostEstimate(flops=9_000_000_000, bytes_accessed=28 << 20, transcendentals=0),
    )(*scalars, current, *pieces, *sources)


def spread(side, quarter, x, low):
    root = lambda a, b, c: a == 0 and b == 0 and c == side
    plane = lambda a, b, c: b == 0 and c == side
    lane = lambda a, b, c: c == side
    from_root = (
        shifted(quarter[1], x=1, keep=root)
        + shifted(quarter[3], x=-1, keep=root)
        + shifted(quarter[2], x=2, keep=root)
    )
    own = jnp.where(x == 0, quarter[0], from_root)
    own = jnp.where(low == 0, own, shifted(own, low=1, keep=plane))
    after = shifted(own, x=-1, keep=lane)
    before = shifted(own, x=1, keep=lane)
    across = shifted(own, x=2, keep=lane)
    return [own, after, across, before]


def shards(right_sides, panel_diag, left_factor, right_factor, tile_scale, tile_rank):
    rows, _ = right_sides.shape
    count = rows // SIZE
    row = lax.axis_index("row")
    col = lax.axis_index("rhs")
    x, low, core = row // 4, (row // 2) % 2, row % 2
    y, high = col // 2, col % 2
    place = jnp.stack([x, low, core, y, high, row]).astype(jnp.int32)

    left_lanes = jnp.transpose(right_factor, (1, 2, 0)).reshape(TILE, count, 4, TILE)
    left_lanes = jnp.transpose(left_lanes, (1, 2, 0, 3)).reshape(count, SIZE, TILE)
    packed = jnp.concatenate([left_lanes, left_factor.reshape(count, SIZE, TILE)], axis=1)

    def lone(factor):
        return jnp.transpose(
            jnp.transpose(factor[:SIZE, 0, :], (1, 0)).reshape(64, 4, TILE), (1, 0, 2)
        ).reshape(256, TILE)

    tile = jnp.concatenate([lone(right_factor), lone(left_factor)], axis=0)
    solver = lambda a, b, c: a == 0 and b == 0 and c == 1
    tile = jnp.concatenate([tile, shifted(tile, high=1, keep=solver)], axis=0)
    turns = (1, 3, 2)
    tiles = [tile] + [shifted(tile, y=dy, keep=solver) for dy in turns]
    tile_places = [((4 - dy) % 4, dh) for dy in (0, *turns) for dh in (0, 1)]

    up = shifted(packed, y=1)
    down = shifted(packed, y=-1)
    over = shifted(packed, high=1)
    over_up = shifted(over, y=1)
    over_down = shifted(over, y=-1)
    far = shifted(up, y=1)
    over_far = shifted(over_down, y=-1)
    pieces = [packed, up, down, over, over_up, over_down, far, over_far]
    places = [(0, 0), (3, 0), (1, 0), (0, 1), (3, 1), (1, 1), (2, 0), (2, 1)]

    right = [right_sides[TILE * k : TILE * k + TILE] for k in range(4)]
    near = [shifted(quarter, core=1, keep=lambda a, b, c: a == 0 and b == 0 and c == 0) for quarter in right]
    inverse = inverses(panel_diag)
    scalars = (place, tile_scale.T, tile_rank.T)
    first = first_solution(place, inverse, spread(0, right, x, low))
    first_core = shifted(first, core=1)
    middle = update(0, scalars, places, right_sides, pieces, [first, first_core])
    quarters = second_solution(scalars, tile_places, inverse, near, right_sides, tiles)
    second = put_in_place(place, spread(1, quarters, x, low))
    second_core = shifted(second, core=1)
    return update(1, scalars, places, middle, pieces, [second, second_core])


def solution(mesh):
    placed = (
        P("row", "rhs"),
        P(),
        P("row", None, "rhs"),
        P("row", None, "rhs"),
        P("row", None),
        P("row", None),
    )
    return jax.shard_map(shards, mesh=mesh, in_specs=placed, out_specs=P("row", "rhs"), check_vma=False)
```

time: 373 us -> 204 us (0.55)
  the two profiles are of different devices: /device:TPU:1 before, /device:TPU:3 now
where the time goes in v1:
time: 204 us; the launch traced here: 203 us
  waiting for transfers between devices  87.9 us (43%)
  Pallas kernels  52.9 us (26%)
  starting transfers between devices  45.2 us (22%)
  local copies, waits for them, and re-layouts  9.85 us (5%)
  other arithmetic  6.37 us (3%)
    ppermute x31, waiting for transfers between devices, shifted(): return lax.ppermute(value, BOTH, moves((x, low, core, y, high), keep))  87.9 us
    ppermute x31, starting transfers between devices, shifted(): return lax.ppermute(value, BOTH, moves((x, low, core, y, high), keep))  45.2 us
    pallas_call x2, Pallas kernels, update(): pl.pallas_call(functools.partial(update_kernel, panel, shifts), grid=(row...  32.2 us
    pallas_call x1, Pallas kernels, inverses(): pl.pallas_call(invert_kernel, out_shape=jax.ShapeDtypeStruct(panel_diag.s...  12.7 us
    pallas_call x1, Pallas kernels, second_solution(): pl.pallas_call(functools.partial(second_kernel, shifts), grid=(width // S...  4.12 us
  transfers between devices with their start and end apart: 31, of which 9 were waited for; matrix products, arithmetic and copies ran while one was open for 6% of the time, Pallas kernels for 16%

profile of v1, /device:TPU:3, one launch (start us, length us, event | category | flops | bytes accessed | tf_op | source)
XLA Modules:
  0.0 202.7 jit_solution(107440141604972651)
XLA Ops:
  0.0 2.6 %fusion.1 = (f32[128,1024]{1,0:T(8,128)}, f32[128,1024]{1,0:T(8,128)}, f32[128,1024]{1,0:T(8,128)}) fusion(f32[2048,1024]{1,0:T(8,128)} %b_ref.3), kind=kLoop, calls=%fused_computation.12 | loop fusion | bytes 3145728 | tf_op jit(solution)/shard_map/slice | solution.py:368
  2.6 0.7 collective-permute-start.8
  3.3 0.7 collective-permute-start.9
  4.0 0.7 collective-permute-start.7
  4.7 0.9 copy_bitcast_fusion
  5.5 0.9 copy_bitcast_fusion.1
  6.4 0.7 collective-permute-start.19
  7.1 1.5 collective-permute-start.18
  8.6 1.5 collective-permute-start.17
  10.0 0.7 pad_maximum_fusion.1.refs_4_
  10.7 1.5 collective-permute-start.16
  12.2 1.4 collective-permute-start.22
  13.6 1.4 collective-permute-start.21
  14.9 2.1 %fusion = (f32[128,1024]{1,0:T(8,128)}, f32[128,1024]{1,0:T(8,128)}) fusion(f32[2048,1024]{1,0:T(8,128)} %b_ref.3, f32[128,1024]{1,0:T(8,128)S(1)} %collective-permute-done.9, f32[128,1024]{1,0:T(8,128)S(1)} %collective-permute-done.7, f32[128,1024]{1,0:T(8,128)S(1)} %collective-permute-done.8, pred[]{:T(512)S(6)} %eq.13), kind=kLoop, calls=%fused_computation.11 | loop fusion | flops 393216 | bytes 3145729 | tf_op jit(solution)/shard_map/slice | solution.py:368
  17.1 0.0 collective-permute-done.22.refs_7_
  17.1 1.5 collective-permute-start.15
  18.5 0.0 collective-permute-done.21.refs_6_
  18.5 1.3 collective-permute-start.20
  19.9 0.6 stack.27.place_ref
  20.5 12.7 %inverses.1.inverse.d_ref = f32[2,512,512]{2,1,0:T(8,128)} custom-call(f32[2,512,512]{2,1,0:T(8,128)} %d_ref.1), custom_call_target="tpu_custom_call" | custom-call | flops 2000000000 | bytes 4194304 | tf_op jit(solution)/shard_map/inverses/pallas_call | solution.py:112
  33.2 0.0 collective-permute-done.16.refs_1_
  33.2 4.1 %second_solution.1 = (f32[128,1024]{1,0:T(8,128)}, f32[128,1024]{1,0:T(8,128)}, f32[128,1024]{1,0:T(8,128)}, f32[128,1024]{1,0:T(8,128)}) custom-call(s32[6]{0:T(128)} %stack.27.place_ref, f32[2,4]{1,0:T(2,128)} %bitcast.42, s32[2,4]{1,0:T(2,128)} %bitcast.45, f32[2,512,512]{2,1,0:T(8,128)} %inverses.1.inverse.d_ref, f32[2048,1024]{1,0:T(8,128)} %b_ref.3, ...), custom_call_target="tpu_custom_call" | custom-call | flops 4000000000 | bytes 9437184 | tf_op jit(solution)/shard_map/second_solution/pallas_call | solution.py:223
  37.3 1.3 collective-permute-start.23
  38.6 1.5 collective-permute-start.24
  40.1 1.6 collective-permute-start.25
  41.7 1.4 reshape.23
  43.1 1.4 reshape.21
  44.5 0.1 copy.11
  44.7 0.4 copy.12
  45.1 0.7 collective-permute-start.10
  45.8 18.5 %collective-permute-done.23 = f32[128,1024]{1,0:T(8,128)} collective-permute-done((f32[128,1024]{1,0:T(8,128)}, f32[128,1024]{1,0:T(8,128)}, u32[]{:S(2)}, u32[]{:S(2)}) %collective-permute-start.23) | collective-permute-done | bytes 524320 | tf_op jit(solution)/shard_map/ppermute | solution.py:38
  64.3 1.5 add_select_fusion
  65.8 1.3 collective-permute-start.26
  67.1 1.0 pad_maximum_fusion.refs_0_
  68.2 3.0 %collective-permute-start.2 = (bf16[4,1024,128]{2,1,0:T(8,128)(2,1)}, bf16[4,1024,128]{2,1,0:T(8,128)(2,1)}, u32[]{:S(2)}, u32[]{:S(2)}) collective-permute-start(bf16[4,1024,128]{2,1,0:T(8,128)(2,1)} %pad_maximum_fusion.refs_0_), channel_id=1, source_target_pairs={{0,1},{1,0},{2,3},{3,2},{4,5},{5,4},{6,7},{7,6},{8,9},{9,8},{10,11... | collective-permute-start | bytes 3145736 | tf_op jit(solution)/shard_map/ppermute | solution.py:38
  71.1 0.1 broadcast_select_fusion.1.refs_0_
  71.2 0.7 collective-permute-start.13
  71.9 0.7 collective-permute-start.12
  72.6 0.7 collective-permute-start.11
  73.3 5.5 %collective-permute-done.26 = f32[128,1024]{1,0:T(8,128)S(1)} collective-permute-done((f32[128,1024]{1,0:T(8,128)S(1)}, f32[128,1024]{1,0:T(8,128)S(1)}, u32[]{:S(2)}, u32[]{:S(2)}) %collective-permute-start.26) | collective-permute-done | bytes 524320 | tf_op jit(solution)/shard_map/ppermute | solution.py:38
  78.8 0.9 broadcast_select_fusion.refs_0_
  79.7 4.8 %collective-permute-start.29 = (f32[128,1024]{1,0:T(8,128)}, f32[128,1024]{1,0:T(8,128)}, u32[]{:S(2)}, u32[]{:S(2)}) collective-permute-start(f32[128,1024]{1,0:T(8,128)} %broadcast_select_fusion.refs_0_), channel_id=1, source_target_pairs={{8,40},{9,41},{10,42},{11,43},{12,44},{13,45},{14,46},{15,47},{24,... | collective-permute-start | bytes 1572872 | tf_op jit(solution)/shard_map/ppermute | solution.py:38
  84.5 9.7 %collective-permute-done.2.refs_3_ = bf16[4,1024,128]{2,1,0:T(8,128)(2,1)} collective-permute-done((bf16[4,1024,128]{2,1,0:T(8,128)(2,1)}, bf16[4,1024,128]{2,1,0:T(8,128)(2,1)}, u32[]{:S(2)}, u32[]{:S(2)}) %collective-permute-start.2) | collective-permute-done | bytes 1048608 | tf_op jit(solution)/shard_map/ppermute | solution.py:38
  94.2 1.9 collective-permute-start.28
  96.2 2.8 %collective-permute-start.1 = (bf16[4,1024,128]{2,1,0:T(8,128)(2,1)}, bf16[4,1024,128]{2,1,0:T(8,128)(2,1)}, u32[]{:S(2)}, u32[]{:S(2)}) collective-permute-start(bf16[4,1024,128]{2,1,0:T(8,128)(2,1)} %pad_maximum_fusion.refs_0_), channel_id=1, source_target_pairs={{0,6},{1,7},{2,0},{3,1},{4,2},{5,3},{6,4},{7,5},{8,14},{9,15},{10,... | collective-permute-start | bytes 3145736 | tf_op jit(solution)/shard_map/ppermute | solution.py:38
  99.0 0.8 copy-done.3
  99.8 0.8 copy-done.4
  100.6 1.9 collective-permute-start.4
  102.5 0.7 first_solution.1.refs_8_
  103.2 0.1 collective-permute-start.14
  103.3 2.9 %collective-permute-done.28.refs_2_ = f32[128,1024]{1,0:T(8,128)} collective-permute-done((f32[128,1024]{1,0:T(8,128)}, f32[128,1024]{1,0:T(8,128)}, u32[]{:S(2)}, u32[]{:S(2)}) %collective-permute-start.28) | collective-permute-done | bytes 524320 | tf_op jit(solution)/shard_map/ppermute | solution.py:38
  106.3 4.0 %collective-permute-start.27 = (f32[128,1024]{1,0:T(8,128)}, f32[128,1024]{1,0:T(8,128)}, u32[]{:S(2)}, u32[]{:S(2)}) collective-permute-start(f32[128,1024]{1,0:T(8,128)} %broadcast_select_fusion.refs_0_), channel_id=1, source_target_pairs={{8,104},{9,105},{10,106},{11,107},{12,108},{13,109},{14,110},{15,1... | collective-permute-start | bytes 1572872 | tf_op jit(solution)/shard_map/ppermute | solution.py:38
  110.3 6.9 %collective-permute-done.27.refs_1_ = f32[128,1024]{1,0:T(8,128)} collective-permute-done((f32[128,1024]{1,0:T(8,128)}, f32[128,1024]{1,0:T(8,128)}, u32[]{:S(2)}, u32[]{:S(2)}) %collective-permute-start.27) | collective-permute-done | bytes 524320 | tf_op jit(solution)/shard_map/ppermute | solution.py:38
  117.1 3.2 %placed.1.refs_8_ = f32[512,1024]{1,0:T(8,128)} custom-call(s32[6]{0:T(128)} %stack.27.place_ref, f32[128,1024]{1,0:T(8,128)} %broadcast_select_fusion.refs_0_, f32[128,1024]{1,0:T(8,128)} %collective-permute-done.27.refs_1_, f32[128,1024]{1,0:T(8,128)} %collective-permute-done.28.refs_2_, f32[128,1024]{1,0:T(8,128)} %collective-permute-done.29.refs_3_), custom_call_target="tpu_custom_call" | custom-call | bytes 4194304 | tf_op jit(solution)/shard_map/placed/pallas_call | solution.py:184
  120.3 0.1 collective-permute-start.30
  120.4 1.9 collective-permute-done.1.refs_2_
  122.3 0.8 collective-permute-start.3
  123.0 1.3 collective-permute-start.5
  124.3 15.3 %collective-permute-done.4.refs_5_ = bf16[4,1024,128]{2,1,0:T(8,128)(2,1)} collective-permute-done((bf16[4,1024,128]{2,1,0:T(8,128)(2,1)}, bf16[4,1024,128]{2,1,0:T(8,128)(2,1)}, u32[]{:S(2)}, u32[]{:S(2)}) %collective-permute-start.4) | collective-permute-done | bytes 1048608 | tf_op jit(solution)/shard_map/ppermute | solution.py:38
  139.7 3.4 %collective-permute-start.6 = (bf16[4,1024,128]{2,1,0:T(8,128)(2,1)}, bf16[4,1024,128]{2,1,0:T(8,128)(2,1)}, u32[]{:S(2)}, u32[]{:S(2)}) collective-permute-start(bf16[4,1024,128]{2,1,0:T(8,128)(2,1)} %collective-permute-done.4.refs_5_), channel_id=1, source_target_pairs={{0,6},{1,7},{2,0},{3,1},{4,2},{5,3},{6,4},{7,5},{8,14},{9,15},{10,... | collective-permute-start | bytes 3145736 | tf_op jit(solution)/shard_map/ppermute | solution.py:38
  143.1 6.6 %collective-permute-done.3.refs_4_ = bf16[4,1024,128]{2,1,0:T(8,128)(2,1)} collective-permute-done((bf16[4,1024,128]{2,1,0:T(8,128)(2,1)}, bf16[4,1024,128]{2,1,0:T(8,128)(2,1)}, u32[]{:S(2)}, u32[]{:S(2)}) %collective-permute-start.3) | collective-permute-done | bytes 1048608 | tf_op jit(solution)/shard_map/ppermute | solution.py:38
  149.7 20.5 %collective-permute-done.5.refs_6_ = bf16[4,1024,128]{2,1,0:T(8,128)(2,1)} collective-permute-done((bf16[4,1024,128]{2,1,0:T(8,128)(2,1)}, bf16[4,1024,128]{2,1,0:T(8,128)(2,1)}, u32[]{:S(2)}, u32[]{:S(2)}) %collective-permute-start.5) | collective-permute-done | bytes 1048608 | tf_op jit(solution)/shard_map/ppermute | solution.py:38
  170.3 16.2 %shard_map.64.b_ref = f32[2048,1024]{1,0:T(8,128)} custom-call(s32[6]{0:T(128)} %stack.27.place_ref, f32[2,4]{1,0:T(2,128)} %bitcast.43, s32[2,4]{1,0:T(2,128)} %bitcast.46, f32[2048,1024]{1,0:T(8,128)} %b_ref.3, bf16[4,1024,128]{2,1,0:T(8,128)(2,1)} %pad_maximum_fusion.refs_0_, bf16[4,1024,128]{2,1,0:T(8,128)(2,1)} %collective-permute-done.refs_1_, ...), custom_call_target="tpu_custom_call" | custom-call | flops 8999999488 | bytes 29360128 | tf_op jit(solution)/shard_map/pallas_call | solution.py:296
  186.4 16.1 %shard_map.65 = f32[2048,1024]{1,0:T(8,128)} custom-call(s32[6]{0:T(128)} %stack.27.place_ref, f32[2,4]{1,0:T(2,128)} %bitcast.44, s32[2,4]{1,0:T(2,128)} %bitcast.47, f32[2048,1024]{1,0:T(8,128)} %shard_map.64.b_ref, bf16[4,1024,128]{2,1,0:T(8,128)(2,1)} %pad_maximum_fusion.refs_0_, bf16[4,1024,128]{2,1,0:T(8,128)(2,1)} %collective-permute-done.refs_1_, ...), custom_call_target="tpu_custom_call" | custom-call | flops 8999999488 | bytes 29360128 | tf_op jit(solution)/shard_map/pallas_call | solution.py:296
  (31 shorter events, 0.1 us)
Async XLA Ops:
  2.6 8.2 %collective-permute-start.8 = (f32[128,1024]{1,0:T(8,128)}, f32[128,1024]{1,0:T(8,128)S(1)}, u32[]{:S(2)}, u32[]{:S(2)}) collective-permute-start(f32[128,1024]{1,0:T(8,128)} %get-tuple-element.15), channel_id=1, source_target_pairs={{0,96},{1,97},{2,98},{3,99},{4,100},{5,101},{6,102},{7,103}} | collective-permute-start | bytes 1572872 | tf_op jit(solution)/shard_map/ppermute | solution.py:38
  3.3 8.9 %collective-permute-start.9 = (f32[128,1024]{1,0:T(8,128)}, f32[128,1024]{1,0:T(8,128)S(1)}, u32[]{:S(2)}, u32[]{:S(2)}) collective-permute-start(f32[128,1024]{1,0:T(8,128)} %get-tuple-element.16), channel_id=1, source_target_pairs={{0,64},{1,65},{2,66},{3,67},{4,68},{5,69},{6,70},{7,71}} | collective-permute-start | bytes 1572872 | tf_op jit(solution)/shard_map/ppermute | solution.py:38
  4.0 9.6 %collective-permute-start.7 = (f32[128,1024]{1,0:T(8,128)}, f32[128,1024]{1,0:T(8,128)S(1)}, u32[]{:S(2)}, u32[]{:S(2)}) collective-permute-start(f32[128,1024]{1,0:T(8,128)} %get-tuple-element.17), channel_id=1, source_target_pairs={{0,32},{1,33},{2,34},{3,35},{4,36},{5,37},{6,38},{7,39}} | collective-permute-start | bytes 1572872 | tf_op jit(solution)/shard_map/ppermute | solution.py:38
  6.4 2.2 %collective-permute-start.19 = (bf16[512,128]{1,0:T(8,128)(2,1)S(1)}, bf16[512,128]{1,0:T(8,128)(2,1)S(1)}, u32[]{:S(2)}, u32[]{:S(2)}) collective-permute-start(bf16[512,128]{1,0:T(8,128)(2,1)S(1)} %pad_maximum_fusion.2), channel_id=1, source_target_pairs={{8,9},{9,8},{10,11},{11,10},{12,13},{13,12},{14,15},{15,14}} | collective-permute-start | bytes 393224 | tf_op jit(solution)/shard_map/ppermute | solution.py:38
  7.1 26.1 %collective-permute-start.18 = (f32[128,1024]{1,0:T(8,128)}, f32[128,1024]{1,0:T(8,128)}, u32[]{:S(2)}, u32[]{:S(2)}) collective-permute-start(f32[128,1024]{1,0:T(8,128)} %get-tuple-element.15), channel_id=1, source_target_pairs={{0,8},{1,9},{2,10},{3,11},{4,12},{5,13},{6,14},{7,15}} | collective-permute-start | bytes 1572872 | tf_op jit(solution)/shard_map/ppermute | solution.py:38
  8.6 24.6 %collective-permute-start.17 = (f32[128,1024]{1,0:T(8,128)}, f32[128,1024]{1,0:T(8,128)}, u32[]{:S(2)}, u32[]{:S(2)}) collective-permute-start(f32[128,1024]{1,0:T(8,128)} %get-tuple-element.16), channel_id=1, source_target_pairs={{0,8},{1,9},{2,10},{3,11},{4,12},{5,13},{6,14},{7,15}} | collective-permute-start | bytes 1572872 | tf_op jit(solution)/shard_map/ppermute | solution.py:38
  10.7 22.4 %collective-permute-start.16 = (f32[128,1024]{1,0:T(8,128)}, f32[128,1024]{1,0:T(8,128)}, u32[]{:S(2)}, u32[]{:S(2)}) collective-permute-start(f32[128,1024]{1,0:T(8,128)} %get-tuple-element.17), channel_id=1, source_target_pairs={{0,8},{1,9},{2,10},{3,11},{4,12},{5,13},{6,14},{7,15}} | collective-permute-start | bytes 1572872 | tf_op jit(solution)/shard_map/ppermute | solution.py:38
  12.2 4.9 %collective-permute-start.22 = (bf16[1024,128]{1,0:T(8,128)(2,1)}, bf16[1024,128]{1,0:T(8,128)(2,1)}, u32[]{:S(2)}, u32[]{:S(2)}) collective-permute-start(bf16[1024,128]{1,0:T(8,128)(2,1)} %pad_maximum_fusion.1.refs_4_), channel_id=1, source_target_pairs={{8,12},{9,13},{10,14},{11,15},{12,8},{13,9},{14,10},{15,11}} | collective-permute-start | bytes 786440 | tf_op jit(solution)/shard_map/ppermute | solution.py:38
  13.6 5.0 %collective-permute-start.21 = (bf16[1024,128]{1,0:T(8,128)(2,1)}, bf16[1024,128]{1,0:T(8,128)(2,1)}, u32[]{:S(2)}, u32[]{:S(2)}) collective-permute-start(bf16[1024,128]{1,0:T(8,128)(2,1)} %pad_maximum_fusion.1.refs_4_), channel_id=1, source_target_pairs={{8,14},{9,15},{10,8},{11,9},{12,10},{13,11},{14,12},{15,13}} | collective-permute-start | bytes 786440 | tf_op jit(solution)/shard_map/ppermute | solution.py:38
  17.1 16.1 %collective-permute-start.15 = (f32[128,1024]{1,0:T(8,128)}, f32[128,1024]{1,0:T(8,128)}, u32[]{:S(2)}, u32[]{:S(2)}) collective-permute-start(f32[128,1024]{1,0:T(8,128)} %get-tuple-element.13), channel_id=1, source_target_pairs={{0,8},{1,9},{2,10},{3,11},{4,12},{5,13},{6,14},{7,15}} | collective-permute-start | bytes 1572872 | tf_op jit(solution)/shard_map/ppermute | solution.py:38
  18.5 14.6 %collective-permute-start.20 = (bf16[1024,128]{1,0:T(8,128)(2,1)}, bf16[1024,128]{1,0:T(8,128)(2,1)}, u32[]{:S(2)}, u32[]{:S(2)}) collective-permute-start(bf16[1024,128]{1,0:T(8,128)(2,1)} %pad_maximum_fusion.1.refs_4_), channel_id=1, source_target_pairs={{8,10},{9,11},{10,12},{11,13},{12,14},{13,15},{14,8},{15,9}} | collective-permute-start | bytes 786440 | tf_op jit(solution)/shard_map/ppermute | solution.py:38
  37.3 27.0 %collective-permute-start.23 = (f32[128,1024]{1,0:T(8,128)}, f32[128,1024]{1,0:T(8,128)}, u32[]{:S(2)}, u32[]{:S(2)}) collective-permute-start(f32[128,1024]{1,0:T(8,128)} %get-tuple-element.10), channel_id=1, source_target_pairs={{8,40},{9,41},{10,42},{11,43},{12,44},{13,45},{14,46},{15,47}} | collective-permute-start | bytes 1572872 | tf_op jit(solution)/shard_map/ppermute | solution.py:38
  38.6 25.7 %collective-permute-start.24 = (f32[128,1024]{1,0:T(8,128)}, f32[128,1024]{1,0:T(8,128)}, u32[]{:S(2)}, u32[]{:S(2)}) collective-permute-start(f32[128,1024]{1,0:T(8,128)} %get-tuple-element.11), channel_id=1, source_target_pairs={{8,104},{9,105},{10,106},{11,107},{12,108},{13,109},{14,110},{15,1... | collective-permute-start | bytes 1572872 | tf_op jit(solution)/shard_map/ppermute | solution.py:38
  40.1 5.0 %copy-start.1 = (f32[128,1024]{1,0:T(8,128)S(1)}, f32[128,1024]{1,0:T(8,128)}, u32[]{:S(2)}) copy-start(f32[128,1024]{1,0:T(8,128)} %get-tuple-element.14) | copy-start | bytes 1572868
  40.1 24.2 %copy-start.5 = (f32[128,1024]{1,0:T(8,128)S(1)}, f32[128,1024]{1,0:T(8,128)}, u32[]{:S(2)}) copy-start(f32[128,1024]{1,0:T(8,128)} %get-tuple-element.9) | copy-start | bytes 1572868
  40.1 24.2 %collective-permute-start.25 = (f32[128,1024]{1,0:T(8,128)}, f32[128,1024]{1,0:T(8,128)}, u32[]{:S(2)}, u32[]{:S(2)}) collective-permute-start(f32[128,1024]{1,0:T(8,128)} %get-tuple-element.12), channel_id=1, source_target_pairs={{8,72},{9,73},{10,74},{11,75},{12,76},{13,77},{14,78},{15,79}} | collective-permute-start | bytes 1572872 | tf_op jit(solution)/shard_map/ppermute | solution.py:38
  45.1 26.0 %collective-permute-start.10 = (f32[128,1024]{1,0:T(8,128)S(1)}, f32[128,1024]{1,0:T(8,128)S(1)}, u32[]{:S(2)}, u32[]{:S(2)}) collective-permute-start(f32[128,1024]{1,0:T(8,128)S(1)} %copy-done.1), channel_id=1, source_target_pairs={{0,16},{1,17},{2,18},{3,19},{4,20},{5,21},{6,22},{7,23},{32,48},{3... | collective-permute-start | bytes 1572872 | tf_op jit(solution)/shard_map/ppermute | solution.py:38
  65.8 13.0 %collective-permute-start.26 = (f32[128,1024]{1,0:T(8,128)S(1)}, f32[128,1024]{1,0:T(8,128)S(1)}, u32[]{:S(2)}, u32[]{:S(2)}) collective-permute-start(f32[128,1024]{1,0:T(8,128)S(1)} %add_select_fusion), channel_id=1, source_target_pairs={{8,24},{9,25},{10,26},{11,27},{12,28},{13,29},{14,30},{15,31},{40,... | collective-permute-start | bytes 1572872 | tf_op jit(solution)/shard_map/ppermute | solution.py:38
  68.2 26.1 %collective-permute-start.2 = (bf16[4,1024,128]{2,1,0:T(8,128)(2,1)}, bf16[4,1024,128]{2,1,0:T(8,128)(2,1)}, u32[]{:S(2)}, u32[]{:S(2)}) collective-permute-start(bf16[4,1024,128]{2,1,0:T(8,128)(2,1)} %pad_maximum_fusion.refs_0_), channel_id=1, source_target_pairs={{0,1},{1,0},{2,3},{3,2},{4,5},{5,4},{6,7},{7,6},{8,9},{9,8},{10,11... | collective-permute-start | bytes 3145736 | tf_op jit(solution)/shard_map/ppermute | solution.py:38
  71.2 1.4 copy-start
  71.2 24.9 %collective-permute-start.13 = (f32[128,1024]{1,0:T(8,128)S(1)}, f32[128,1024]{1,0:T(8,128)S(1)}, u32[]{:S(2)}, u32[]{:S(2)}) collective-permute-start(f32[128,1024]{1,0:T(8,128)S(1)} %broadcast_select_fusion.1.refs_0_), channel_id=1, source_target_pairs={{0,32},{1,33},{2,34},{3,35},{4,36},{5,37},{6,38},{7,39},{16,48},{1... | collective-permute-start | bytes 1572872 | tf_op jit(solution)/shard_map/ppermute | solution.py:38
  71.9 27.1 %collective-permute-start.12 = (f32[128,1024]{1,0:T(8,128)S(1)}, f32[128,1024]{1,0:T(8,128)S(1)}, u32[]{:S(2)}, u32[]{:S(2)}) collective-permute-start(f32[128,1024]{1,0:T(8,128)S(1)} %broadcast_select_fusion.1.refs_0_), channel_id=1, source_target_pairs={{0,64},{1,65},{2,66},{3,67},{4,68},{5,69},{6,70},{7,71},{16,80},{1... | collective-permute-start | bytes 1572872 | tf_op jit(solution)/shard_map/ppermute | solution.py:38
  72.6 26.4 %collective-permute-start.11 = (f32[128,1024]{1,0:T(8,128)S(1)}, f32[128,1024]{1,0:T(8,128)S(1)}, u32[]{:S(2)}, u32[]{:S(2)}) collective-permute-start(f32[128,1024]{1,0:T(8,128)S(1)} %broadcast_select_fusion.1.refs_0_), channel_id=1, source_target_pairs={{0,96},{1,97},{2,98},{3,99},{4,100},{5,101},{6,102},{7,103},{16,11... | collective-permute-start | bytes 1572872 | tf_op jit(solution)/shard_map/ppermute | solution.py:38
  79.7 23.5 %collective-permute-start.29 = (f32[128,1024]{1,0:T(8,128)}, f32[128,1024]{1,0:T(8,128)}, u32[]{:S(2)}, u32[]{:S(2)}) collective-permute-start(f32[128,1024]{1,0:T(8,128)} %broadcast_select_fusion.refs_0_), channel_id=1, source_target_pairs={{8,40},{9,41},{10,42},{11,43},{12,44},{13,45},{14,46},{15,47},{24,... | collective-permute-start | bytes 1572872 | tf_op jit(solution)/shard_map/ppermute | solution.py:38
  94.2 12.0 %collective-permute-start.28 = (f32[128,1024]{1,0:T(8,128)}, f32[128,1024]{1,0:T(8,128)}, u32[]{:S(2)}, u32[]{:S(2)}) collective-permute-start(f32[128,1024]{1,0:T(8,128)} %broadcast_select_fusion.refs_0_), channel_id=1, source_target_pairs={{8,72},{9,73},{10,74},{11,75},{12,76},{13,77},{14,78},{15,79},{24,... | collective-permute-start | bytes 1572872 | tf_op jit(solution)/shard_map/ppermute | solution.py:38
  96.2 2.8 %copy-start.2 = (f32[128,1024]{1,0:T(8,128)}, f32[128,1024]{1,0:T(8,128)S(1)}, u32[]{:S(2)}) copy-start(f32[128,1024]{1,0:T(8,128)S(1)} %collective-permute-done.13.refs_3_) | copy-start | bytes 1572868
  96.2 26.1 %collective-permute-start.1 = (bf16[4,1024,128]{2,1,0:T(8,128)(2,1)}, bf16[4,1024,128]{2,1,0:T(8,128)(2,1)}, u32[]{:S(2)}, u32[]{:S(2)}) collective-permute-start(bf16[4,1024,128]{2,1,0:T(8,128)(2,1)} %pad_maximum_fusion.refs_0_), channel_id=1, source_target_pairs={{0,6},{1,7},{2,0},{3,1},{4,2},{5,3},{6,4},{7,5},{8,14},{9,15},{10,... | collective-permute-start | bytes 3145736 | tf_op jit(solution)/shard_map/ppermute | solution.py:38
  99.0 0.8 copy-start.3
  99.0 24.1 %collective-permute-start = (bf16[4,1024,128]{2,1,0:T(8,128)(2,1)}, bf16[4,1024,128]{2,1,0:T(8,128)(2,1)}, u32[]{:S(2)}, u32[]{:S(2)}) collective-permute-start(bf16[4,1024,128]{2,1,0:T(8,128)(2,1)} %pad_maximum_fusion.refs_0_), channel_id=1, source_target_pairs={{0,2},{1,3},{2,4},{3,5},{4,6},{5,7},{6,0},{7,1},{8,10},{9,11},{10,... | collective-permute-start | bytes 3145736 | tf_op jit(solution)/shard_map/ppermute | solution.py:38
  99.8 0.8 copy-start.4
  100.6 39.1 %collective-permute-start.4 = (bf16[4,1024,128]{2,1,0:T(8,128)(2,1)}, bf16[4,1024,128]{2,1,0:T(8,128)(2,1)}, u32[]{:S(2)}, u32[]{:S(2)}) collective-permute-start(bf16[4,1024,128]{2,1,0:T(8,128)(2,1)} %collective-permute-done.2.refs_3_), channel_id=1, source_target_pairs={{0,6},{1,7},{2,0},{3,1},{4,2},{5,3},{6,4},{7,5},{8,14},{9,15},{10,... | collective-permute-start | bytes 3145736 | tf_op jit(solution)/shard_map/ppermute | solution.py:38
  103.2 67.0 %collective-permute-start.14 = (f32[512,1024]{1,0:T(8,128)}, f32[512,1024]{1,0:T(8,128)}, u32[]{:S(2)}, u32[]{:S(2)}) collective-permute-start(f32[512,1024]{1,0:T(8,128)} %first_solution.1.refs_8_), channel_id=1, source_target_pairs={{0,8},{1,9},{2,10},{3,11},{4,12},{5,13},{6,14},{7,15},{8,0},{9,1},... | collective-permute-start | bytes 6291464 | tf_op jit(solution)/shard_map/ppermute | solution.py:38
  106.3 10.9 %collective-permute-start.27 = (f32[128,1024]{1,0:T(8,128)}, f32[128,1024]{1,0:T(8,128)}, u32[]{:S(2)}, u32[]{:S(2)}) collective-permute-start(f32[128,1024]{1,0:T(8,128)} %broadcast_select_fusion.refs_0_), channel_id=1, source_target_pairs={{8,104},{9,105},{10,106},{11,107},{12,108},{13,109},{14,110},{15,1... | collective-permute-start | bytes 1572872 | tf_op jit(solution)/shard_map/ppermute | solution.py:38
  120.3 66.1 %collective-permute-start.30 = (f32[512,1024]{1,0:T(8,128)}, f32[512,1024]{1,0:T(8,128)}, u32[]{:S(2)}, u32[]{:S(2)}) collective-permute-start(f32[512,1024]{1,0:T(8,128)} %placed.1.refs_8_), channel_id=1, source_target_pairs={{0,8},{1,9},{2,10},{3,11},{4,12},{5,13},{6,14},{7,15},{8,0},{9,1},... | collective-permute-start | bytes 6291464 | tf_op jit(solution)/shard_map/ppermute | solution.py:38
  122.3 27.4 %collective-permute-start.3 = (bf16[4,1024,128]{2,1,0:T(8,128)(2,1)}, bf16[4,1024,128]{2,1,0:T(8,128)(2,1)}, u32[]{:S(2)}, u32[]{:S(2)}) collective-permute-start(bf16[4,1024,128]{2,1,0:T(8,128)(2,1)} %collective-permute-done.2.refs_3_), channel_id=1, source_target_pairs={{0,2},{1,3},{2,4},{3,5},{4,6},{5,7},{6,0},{7,1},{8,10},{9,11},{10,... | collective-permute-start | bytes 3145736 | tf_op jit(solution)/shard_map/ppermute | solution.py:38
  123.0 47.2 %collective-permute-start.5 = (bf16[4,1024,128]{2,1,0:T(8,128)(2,1)}, bf16[4,1024,128]{2,1,0:T(8,128)(2,1)}, u32[]{:S(2)}, u32[]{:S(2)}) collective-permute-start(bf16[4,1024,128]{2,1,0:T(8,128)(2,1)} %collective-permute-done.refs_1_), channel_id=1, source_target_pairs={{0,2},{1,3},{2,4},{3,5},{4,6},{5,7},{6,0},{7,1},{8,10},{9,11},{10,... | collective-permute-start | bytes 3145736 | tf_op jit(solution)/shard_map/ppermute | solution.py:38
  139.7 30.6 %collective-permute-start.6 = (bf16[4,1024,128]{2,1,0:T(8,128)(2,1)}, bf16[4,1024,128]{2,1,0:T(8,128)(2,1)}, u32[]{:S(2)}, u32[]{:S(2)}) collective-permute-start(bf16[4,1024,128]{2,1,0:T(8,128)(2,1)} %collective-permute-done.4.refs_5_), channel_id=1, source_target_pairs={{0,6},{1,7},{2,0},{3,1},{4,2},{5,3},{6,4},{7,5},{8,14},{9,15},{10,... | collective-permute-start | bytes 3145736 | tf_op jit(solution)/shard_map/ppermute | solution.py:38
